TPU v7x, 32 devices: a whole 2x2x4 slice. The times are simulated.
32 devices in a mesh: groups: 2 (over x), level: 16 (over z, y, core).
Axes of the slice: x: 2, y: 2, z: 4, core: 2. Of those that a mesh axis runs over, the one named last changes fastest.
Arguments:
- latents: bfloat16 [64, 256, 640], P(('groups', 'level')), parts along dimension 0, may hold values from -6 to 6
- levels: int32 [64], P(('groups', 'level')), parts along dimension 0, may hold values from 0 to 15
- back_reach: int32 [64], P(('groups', 'level')), parts along dimension 0, may hold values from 1 to 2
- text_ids: int32 [154], P('groups'), parts along dimension 0, may hold values from 0 to 49407
- text_table: bfloat16 [49408, 1024], P('level'), may hold values from -6 to 6
- text_proj: bfloat16 [1024, 640], replicated, may hold values from -0.75 to 0.75
- level_embed: float32 [16, 640], replicated, may hold values from -3 to 3
- step_rate: float32 [16], replicated, may hold values from 0.3 to 1
- norm_gain: float32 [640], replicated, may hold values from 0.5 to 1.5
- w_query: bfloat16 [640, 640], replicated
- w_key: bfloat16 [640, 640], replicated
- w_value: bfloat16 [640, 640], replicated, may hold values from -0.25 to 0.25
- w_out: bfloat16 [640, 640], replicated, may hold values from -0.25 to 0.25
Outputs:
- queue_out: bfloat16 [64, 256, 640], P(('groups', 'level')), parts along dimension 0
There are 2 independent parts, one for each index of `groups`. A program takes and returns all parts, laid end to end along the dimension named above; an argument that names none is the same for every part. Nothing has to cross between parts.
All inputs are finite; a program needn't handle non-finite values.
Results may differ from a plain program's by a relative error of at most 0.007.
Values may be sent and summed in bfloat16 or wider, within the bound.
A program may use at most 64 MiB of HBM per device.

v0:
```python
import functools

import jax
import jax.numpy as jnp
from jax import lax
from jax.experimental import pallas as pl
from jax.experimental.pallas import tpu as pltpu
from jax.sharding import PartitionSpec as P

DH = 64
BAND = 2
STEPS = 3
SPAN = 2 * BAND + 1
MESH = pl.DeviceIdType.MESH


def queue_kernel(
    n,
    blocks,
    x_hbm,
    level_hbm,
    reach_hbm,
    ids_hbm,
    table_hbm,
    proj_hbm,
    embed_hbm,
    srate_hbm,
    gain_hbm,
    wq_hbm,
    wk_hbm,
    wv_hbm,
    wo_hbm,
    out_hbm,
    recv,
    xa,
    xb,
    xo,
    q_s,
    k_even,
    k_odd,
    v_even,
    v_odd,
    table,
    proj,
    embed,
    gain_s,
    wq,
    wk,
    wv,
    wo,
    level_s,
    reach_s,
    ids_s,
    srate_s,
    pool,
    metas,
    cond,
    rate,
    mask,
    fold,
    unfold,
    x_send,
    x_recv,
    p_send,
    p_recv,
    m_send,
    m_recv,
    o_send,
    o_recv,
    local,
):
    me = lax.axis_index("level")
    fdev = x_hbm.shape[0]
    halves, frames, pos, width = recv.shape
    rows = frames * pos
    pad = BAND * pos
    barrier = pltpu.get_barrier_semaphore()
    for hop in range(1, n):
        pl.semaphore_signal(
            barrier, inc=1, device_id={"level": lax.rem(me + hop, n)}, device_id_type=MESH
        )
    mine = pl.ds(me * fdev, fdev)
    pairs = [
        (level_hbm, level_s),
        (reach_hbm, reach_s),
        (ids_hbm, ids_s),
        (srate_hbm, srate_s),
        (table_hbm, table),
        (embed_hbm, embed),
        (gain_hbm, gain_s),
        (proj_hbm, proj),
        (wq_hbm, wq),
        (wk_hbm, wk),
        (wv_hbm, wv),
        (wo_hbm, wo),
    ] + [(x_hbm.at[:, me, h], recv.at[h, mine]) for h in range(halves)]
    stage = [
        pltpu.make_async_copy(src, dst, local.at[slot]) for slot, (src, dst) in enumerate(pairs)
    ]
    for copy in stage:
        copy.start()

    def x_copy(h, peer, owner):
        return pltpu.make_async_remote_copy(
            src_ref=x_hbm.at[:, peer, h],
            dst_ref=recv.at[h, pl.ds(owner * fdev, fdev)],
            send_sem=x_send.at[h, peer],
            recv_sem=x_recv.at[h, owner],
            device_id={"level": peer},
            device_id_type=MESH,
        )

    def p_copy(peer, owner):
        return pltpu.make_async_remote_copy(
            src_ref=pool.at[owner],
            dst_ref=pool.at[owner],
            send_sem=p_send.at[peer],
            recv_sem=p_recv.at[owner],
            device_id={"level": peer},
            device_id_type=MESH,
        )

    def m_copy(peer, owner):
        return pltpu.make_async_remote_copy(
            src_ref=metas.at[owner],
            dst_ref=metas.at[owner],
            send_sem=m_send.at[peer],
            recv_sem=m_recv.at[owner],
            device_id={"level": peer},
            device_id_type=MESH,
        )

    def o_copy(h, section, owner, peer):
        return pltpu.make_async_remote_copy(
            src_ref=xo.at[h, pl.ds(section * fdev, fdev)],
            dst_ref=out_hbm.at[:, owner, h],
            send_sem=o_send.at[h, peer],
            recv_sem=o_recv.at[h, owner],
            device_id={"level": peer},
            device_id_type=MESH,
        )

    order = sorted(range(1, n), key=lambda hop: min(hop, n - hop))
    peers = [lax.rem(me + hop, n) for hop in order]
    pl.semaphore_wait(barrier, n - 1)
    early = (n - 1) * 9 // 15
    for peer in peers[:early]:
        x_copy(0, peer, me).start()

    stage[0].wait()
    stage[1].wait()
    lane = lax.broadcasted_iota(jnp.int32, (1, 128), 1)
    fact = jnp.zeros((1, 128), jnp.int32)
    for f in range(fdev):
        fact = jnp.where(lane == f, level_s[f], fact)
        fact = jnp.where(lane == fdev + f, reach_s[f], fact)
    metas[me] = fact
    for peer in peers:
        m_copy(peer, me).start()

    vocab = table.shape[0]
    stage[2].wait()
    first_id = me * vocab
    spots = lax.broadcasted_iota(jnp.int32, (1, vocab), 1) + first_id
    counts = jnp.zeros((1, vocab), jnp.float32)
    text_tokens = ids_s.shape[0]
    for token in range(text_tokens):
        counts = counts + jnp.where(spots == ids_s[token], 1.0, 0.0)
    counts = jnp.broadcast_to(counts, (16, vocab)).astype(jnp.bfloat16)
    stage[4].wait()
    partial = jnp.dot(counts, table[...], preferred_element_type=jnp.float32)
    pool[me] = partial[0:1]
    for peer in peers:
        p_copy(peer, me).start()
    for peer in peers[early:]:
        x_copy(0, peer, me).start()
    for h in range(1, halves):
        for peer in peers:
            x_copy(h, peer, me).start()

    row = lax.broadcasted_iota(jnp.int32, (width, 128), 0)
    col = lax.broadcasted_iota(jnp.int32, (width, 128), 1) * DH
    fold[...] = ((row >= col) & (row < col + DH)).astype(jnp.float32).astype(jnp.bfloat16)
    row = lax.broadcasted_iota(jnp.int32, (128, width), 0) * DH
    col = lax.broadcasted_iota(jnp.int32, (128, width), 1)
    unfold[...] = ((col >= row) & (col < row + DH)).astype(jnp.float32).astype(jnp.bfloat16)
    edge = jnp.zeros((pad, width), jnp.bfloat16)
    for buffer in (k_even, v_even):
        buffer[0:pad] = edge
        buffer[rows + pad : rows + 2 * pad] = edge

    for slot in (3, 5, 6, 7):
        stage[slot].wait()
    for peer in peers:
        m_copy(peer, peer).wait_recv()
    facts = metas[...].reshape(n, 128)
    slot_index = lax.broadcasted_iota(jnp.int32, (n, 128), 0)
    bases = []
    for f in range(fdev):
        level = facts[:, f : f + 1]
        base = jnp.zeros((n, width), jnp.float32)
        speed = jnp.zeros((n, width), jnp.float32)
        for number in range(embed.shape[0]):
            chosen = level == number
            base = base + jnp.where(chosen, embed[number : number + 1, :], 0.0)
            speed = speed + jnp.where(chosen, srate_s[number], 0.0)
        bases.append(base)
        reach = jnp.broadcast_to(facts[:, fdev + f : fdev + f + 1], (n, 128))
        spot = slot_index * fdev + f
        for s in range(n):
            rate[s * fdev + f] = speed[s : s + 1]
        for slot in range(SPAN):
            offset = slot - BAND
            valid = ((reach >= -offset) & (spot + offset >= 0) & (spot + offset < frames)).astype(
                jnp.float32
            )
            for s in range(n):
                mask[slot, s * fdev + f] = valid[s : s + 1]

    for peer in peers:
        p_copy(peer, peer).wait_recv()
    pooled = jnp.sum(pool[...], axis=0) / float(text_tokens)
    pooled = jnp.broadcast_to(pooled, (16, pooled.shape[1])).astype(jnp.bfloat16)
    text = jnp.dot(pooled, proj[...], preferred_element_type=jnp.float32)[0:1]
    for f in range(fdev):
        full = bases[f] + text
        for s in range(n):
            cond[s * fdev + f] = full[s : s + 1]

    for slot in (8, 9, 10, 11):
        stage[slot].wait()

    gain = gain_s[...].reshape(1, 1, width)
    scale = 1.0 / DH**0.5
    group = frames // blocks
    size = group * pos

    def project(current):
        hin = current + cond[...]
        power = jnp.mean(hin * hin, axis=-1, keepdims=True)
        flat = (hin * lax.rsqrt(power + 1e-06) * gain).reshape(rows, width).astype(jnp.bfloat16)
        q_s[...] = jnp.dot(flat, wq[...], preferred_element_type=jnp.float32).astype(jnp.bfloat16)
        fill = jnp.zeros((pos, width), jnp.float32)
        for weight, even, odd in ((wk, k_even, k_odd), (wv, v_even, v_odd)):
            made = jnp.dot(flat, weight[...], preferred_element_type=jnp.float32)
            even[pad : pad + rows] = made.astype(jnp.bfloat16)
            odd[0 : rows + 2 * pos] = jnp.concatenate([fill, made, fill], axis=0).astype(
                jnp.bfloat16
            )

    def attend(first, current):
        at = pl.ds(first, group)
        start = first * pos

        def shifted(even, odd, slot):
            source = even if slot % 2 == 0 else odd
            return source[pl.ds(pl.multiple_of(start + (slot - slot % 2) * pos, 16), size)]

        query = q_s[pl.ds(pl.multiple_of(start, 16), size)]
        scores = []
        masks = []
        for slot in range(SPAN):
            keys = shifted(k_even, k_odd, slot)
            raw = jnp.dot(query * keys, fold[...], preferred_element_type=jnp.float32) * scale
            valid = mask[slot, at]
            scores.append(jnp.where(valid > 0.0, raw.reshape(group, pos, 128), -1e30))
            masks.append(valid)
        top = functools.reduce(jnp.maximum, scores)
        expo = [jnp.exp(score - top) * valid for score, valid in zip(scores, masks)]
        inverse = 1.0 / functools.reduce(jnp.add, expo)
        total = None
        for slot in range(SPAN):
            weight = (expo[slot] * inverse).reshape(size, 128).astype(jnp.bfloat16)
            spread = jnp.dot(weight, unfold[...], preferred_element_type=jnp.float32)
            term = spread * shifted(v_even, v_odd, slot).astype(jnp.float32)
            total = term if total is None else total + term
        noise = jnp.dot(total.astype(jnp.bfloat16), wo[...], preferred_element_type=jnp.float32)
        return current - rate[at] * noise.reshape(group, pos, width)

    def half(h, carry):
        stage_x = pltpu.make_async_copy(x_hbm.at[:, me, h], recv.at[h, mine], local.at[12 + h])
        stage_x.wait()
        for peer in peers:
            x_copy(h, peer, peer).wait_recv()
        turn = fdev * pos
        for step in range(STEPS):
            last = step == STEPS - 1
            held = xa if step % 2 == 1 else xb
            fresh = xb if step % 2 == 1 else xa

            def load(first, count, step=step, held=held):
                if step == 0:
                    return recv[h, pl.ds(first, count)].astype(jnp.float32)
                start = pl.multiple_of(first * pos, 16)
                return (
                    held[pl.ds(start, count * pos)].astype(jnp.float32).reshape(count, pos, width)
                )

            project(load(0, frames))

            def body(index, carry, load=load, fresh=fresh, last=last):
                first = index * group
                made = attend(first, load(first, group))
                if last:
                    xo[h, pl.ds(first, group)] = made.astype(jnp.bfloat16)
                else:
                    spot = pl.multiple_of(first * pos + turn, 16)
                    fresh[pl.ds(spot, size)] = made.reshape(size, width).astype(jnp.bfloat16)
                return carry

            lax.fori_loop(0, blocks, body, 0)
            if not last:
                fresh[0:turn] = fresh[rows : rows + turn]
        for peer in peers:
            o_copy(h, lax.rem(peer + n - 1, n), me, peer).start()
        pltpu.make_async_copy(
            xo.at[h, pl.ds(lax.rem(me + n - 1, n) * fdev, fdev)],
            out_hbm.at[:, me, h],
            local.at[12 + halves + h],
        ).start()
        return carry

    lax.fori_loop(0, halves, half, 0)

    for h in range(halves):
        for peer in peers:
            x_copy(h, peer, me).wait_send()
    for peer in peers:
        m_copy(peer, me).wait_send()
        p_copy(peer, me).wait_send()
    for h in range(halves):
        pltpu.make_async_copy(
            xo.at[h, pl.ds(lax.rem(me + n - 1, n) * fdev, fdev)],
            out_hbm.at[:, me, h],
            local.at[12 + halves + h],
        ).wait()
        for peer in peers:
            o_copy(h, lax.rem(peer + n - 1, n), me, peer).wait_send()
            o_copy(h, lax.rem(me + n - 1, n), peer, me).wait_recv()


HALVES = 2
BLOCKS = 1
GRANT = 40 << 20


def fused(
    latents,
    levels,
    back_reach,
    text_ids,
    text_table,
    text_proj,
    level_embed,
    step_rate,
    norm_gain,
    w_query,
    w_key,
    w_value,
    w_out,
):
    n = lax.axis_size("level")
    fdev, tokens, width = latents.shape
    pos = tokens // (n * HALVES)
    frames = fdev * n
    rows = frames * pos
    bf16, f32, i32 = jnp.bfloat16, jnp.float32, jnp.int32
    anywhere = pl.BlockSpec(memory_space=pl.ANY)
    stored = pl.BlockSpec(memory_space=pltpu.HBM)
    dma = pltpu.SemaphoreType.DMA
    block = pltpu.VMEM((HALVES, frames, pos, width), bf16)
    rolled = pltpu.VMEM((rows + fdev * pos, width), bf16)
    padded = pltpu.VMEM((rows + 2 * BAND * pos, width), bf16)
    square = pltpu.VMEM((width, width), bf16)
    out = pl.pallas_call(
        functools.partial(queue_kernel, n, BLOCKS),
        out_shape=jax.ShapeDtypeStruct((fdev, n, HALVES, pos, width), bf16),
        in_specs=[stored] * 13,
        out_specs=anywhere,
        scratch_shapes=[
            block,
            rolled,
            rolled,
            block,
            pltpu.VMEM((rows, width), bf16),
            padded,
            padded,
            padded,
            padded,
            pltpu.VMEM(text_table.shape, bf16),
            pltpu.VMEM(text_proj.shape, bf16),
            pltpu.VMEM(level_embed.shape, f32),
            pltpu.VMEM(norm_gain.shape, f32),
            square,
            square,
            square,
            square,
            pltpu.SMEM(levels.shape, i32),
            pltpu.SMEM(back_reach.shape, i32),
            pltpu.SMEM(text_ids.shape, i32),
            pltpu.SMEM(step_rate.shape, f32),
            pltpu.VMEM((n, 1, text_table.shape[1]), f32),
            pltpu.VMEM((n, 1, 128), i32),
            pltpu.VMEM((frames, 1, width), f32),
            pltpu.VMEM((frames, 1, width), f32),
            pltpu.VMEM((SPAN, frames, 1, 128), f32),
            pltpu.VMEM((width, 128), bf16),
            pltpu.VMEM((128, width), bf16),
            dma((HALVES, n)),
            dma((HALVES, n)),
            dma((n,)),
            dma((n,)),
            dma((n,)),
            dma((n,)),
            dma((HALVES, n)),
            dma((HALVES, n)),
            dma((12 + 2 * HALVES,)),
        ],
        compiler_params=pltpu.CompilerParams(
            collective_id=0, has_side_effects=True, vmem_limit_bytes=GRANT
        ),
        name="queue",
    )(
        *(
            pltpu.with_memory_space_constraint(value, pltpu.HBM)
            for value in (
                latents.reshape(fdev, n, HALVES, pos, width),
                levels,
                back_reach,
                text_ids,
                text_table,
                text_proj,
                level_embed,
                step_rate,
                norm_gain,
                w_query,
                w_key,
                w_value,
                w_out,
            )
        )
    )
    return out.reshape(fdev, tokens, width)


def general(
    latents,
    levels,
    back_reach,
    text_ids,
    text_table,
    text_proj,
    level_embed,
    step_rate,
    norm_gain,
    w_query,
    w_key,
    w_value,
    w_out,
):
    n = lax.axis_size("level")
    index = lax.axis_index("level")
    fdev, tokens, width = latents.shape
    heads = width // DH
    frames = fdev * n
    vocab = text_table.shape[0]
    spots = index * vocab + jnp.arange(vocab, dtype=jnp.int32)
    counts = jnp.sum((text_ids[:, None] == spots[None, :]).astype(jnp.float32), axis=0)
    partial = jnp.dot(
        counts.astype(jnp.bfloat16)[None, :], text_table, preferred_element_type=jnp.float32
    )
    pooled = lax.psum(partial, "level") / text_ids.shape[0]
    text_vec = jnp.dot(pooled.astype(jnp.bfloat16), text_proj, preferred_element_type=jnp.float32)
    levels = lax.all_gather(levels, "level", tiled=True)
    reach = lax.all_gather(back_reach, "level", tiled=True)
    cond = level_embed[levels] + text_vec
    rate = step_rate[levels]
    current = lax.all_to_all(latents, "level", split_axis=1, concat_axis=0, tiled=True)
    pos = tokens // n
    spot = jnp.arange(frames, dtype=jnp.int32)
    for step in range(STEPS):
        hin = current.astype(jnp.float32) + cond[:, None, :]
        power = jnp.mean(hin * hin, axis=-1, keepdims=True)
        normed = (hin * lax.rsqrt(power + 1e-06) * norm_gain).astype(jnp.bfloat16)
        flat = normed.reshape(-1, width)

        def project(weight):
            out = jnp.dot(flat, weight, preferred_element_type=jnp.float32)
            return out.astype(jnp.bfloat16).reshape(frames, pos, heads, DH).astype(jnp.float32)

        edge = ((BAND, BAND), (0, 0), (0, 0), (0, 0))
        query = project(w_query)
        keys = jnp.pad(project(w_key), edge)
        values = jnp.pad(project(w_value), edge)
        scores = []
        masks = []
        for offset in range(-BAND, BAND + 1):
            raw = jnp.sum(query * keys[BAND + offset : BAND + offset + frames], -1) / DH**0.5
            valid = (offset >= -reach) & (spot + offset >= 0) & (spot + offset < frames)
            scores.append(jnp.where(valid[:, None, None], raw, -1e30))
            masks.append(valid.astype(jnp.float32)[:, None, None])
        scores = jnp.stack(scores)
        expo = jnp.exp(scores - jnp.max(scores, axis=0)[None]) * jnp.stack(masks)
        weights = (expo / jnp.sum(expo, axis=0)[None]).astype(jnp.bfloat16).astype(jnp.float32)
        attended = jnp.zeros((frames, pos, heads, DH), jnp.float32)
        for slot in range(SPAN):
            attended = attended + weights[slot][..., None] * values[slot : slot + frames]
        noise = jnp.dot(
            attended.astype(jnp.bfloat16).reshape(-1, width),
            w_out,
            preferred_element_type=jnp.float32,
        ).reshape(frames, pos, width)
        updated = current.astype(jnp.float32) - rate[:, None, None] * noise
        current = jnp.roll(updated.astype(jnp.bfloat16), fdev, axis=0)
    return lax.all_to_all(current, "level", split_axis=0, concat_axis=1, tiled=True)


def per_device(latents, *rest):
    n = lax.axis_size("level")
    tokens = latents.shape[1]
    if tokens % (8 * HALVES * n) == 0 and latents.shape[0] % 2 == 0:
        return fused(latents, *rest)
    return general(latents, *rest)


def solution(mesh):
    in_specs = (
        P(("groups", "level"), None, None),
        P(("groups", "level")),
        P(("groups", "level")),
        P("groups"),
        P("level", None),
        P(),
        P(),
        P(),
        P(),
        P(),
        P(),
        P(),
        P(),
    )
    out_specs = P(("groups", "level"), None, None)
    return jax.shard_map(
        per_device, mesh=mesh, in_specs=in_specs, out_specs=out_specs, check_vma=False
    )
```

profile of v0, /device:TPU:0, one launch (start us, length us, event | category | flops | bytes accessed | tf_op | source)
XLA Modules:
  0.0 44.3 jit_solution(14287303919458992220)
XLA Ops:
  0.0 43.4 %queue.1 = bf16[2,16,2,8,640]{4,3,2,1,0:T(8,128)(2,1)S(1)} custom-call(bf16[2,16,2,8,640]{4,3,2,1,0:T(8,128)(2,1)} %bitcast.3, s32[2]{0:T(128)} %level_hbm.1, s32[2]{0:T(128)} %reach_hbm.1, s32[77]{0:T(128)} %ids_hbm.1, bf16[3088,1024]{1,0:T(8,128)(2,1)} %table_hbm.1, bf16[1024,640]{1,0:T(8,128)(2,1)} %proj_hbm.1, f32[16,640]{1,0:T(8,128)} %embed_hbm.1, ...), custom_call_target="tpu_custom_call" | custom-call | tf_op jit(solution)/shard_map/queue/pallas_call | solution.py:375
  43.4 0.8 %copy.15 = bf16[2,256,640]{2,1,0:T(8,128)(2,1)} copy(bf16[2,256,640]{2,1,0:T(8,128)(2,1)S(1)} %bitcast.2) | data formatting | bytes 1310720
where the time goes:
time: 44.4 us; the launch traced here: 44.3 us
  Pallas kernels  43.4 us (98%)
  local copies, waits for them, and re-layouts  0.84 us (2%)
    pallas_call x1, Pallas kernels, fused(): pl.pallas_call(functools.partial(queue_kernel, n, BLOCKS), out_shape=jax....  43.4 us

commit v1 on v0

--- a/solution.py
+++ b/solution.py
@@ -16,7 +16,6 @@
 
 def queue_kernel(
     n,
-    blocks,
     x_hbm,
     level_hbm,
     reach_hbm,
@@ -36,10 +35,10 @@
     xb,
     xo,
     q_s,
-    k_even,
-    k_odd,
-    v_even,
-    v_odd,
+    k_s,
+    v_s,
+    part,
+    att,
     table,
     proj,
     embed,
@@ -48,6 +47,10 @@
     wk,
     wv,
     wo,
+    wqp,
+    wkp,
+    wvp,
+    wop,
     level_s,
     reach_s,
     ids_s,
@@ -57,8 +60,9 @@
     cond,
     rate,
     mask,
-    fold,
-    unfold,
+    perm,
+    unperm,
+    gather,
     x_send,
     x_recv,
     p_send,
@@ -140,10 +144,17 @@
             device_id_type=MESH,
         )
 
-    order = sorted(range(1, n), key=lambda hop: min(hop, n - hop))
-    peers = [lax.rem(me + hop, n) for hop in order]
+    def flip(bits):
+        other = me
+        for place in range(n.bit_length()):
+            if bits >> place & 1:
+                bit = lax.rem(lax.div(me, 1 << place), 2)
+                other = other + (1 - 2 * bit) * (1 << place)
+        return other
+
+    peers = [flip(bits) for bits in range(1, n)]
     pl.semaphore_wait(barrier, n - 1)
-    early = (n - 1) * 9 // 15
+    early = n // 2
     for peer in peers[:early]:
         x_copy(0, peer, me).start()
 
@@ -178,16 +189,49 @@
         for peer in peers:
             x_copy(h, peer, me).start()
 
-    row = lax.broadcasted_iota(jnp.int32, (width, 128), 0)
-    col = lax.broadcasted_iota(jnp.int32, (width, 128), 1) * DH
-    fold[...] = ((row >= col) & (row < col + DH)).astype(jnp.float32).astype(jnp.bfloat16)
-    row = lax.broadcasted_iota(jnp.int32, (128, width), 0) * DH
-    col = lax.broadcasted_iota(jnp.int32, (128, width), 1)
-    unfold[...] = ((col >= row) & (col < row + DH)).astype(jnp.float32).astype(jnp.bfloat16)
-    edge = jnp.zeros((pad, width), jnp.bfloat16)
-    for buffer in (k_even, v_even):
+    heads = width // DH
+    per = 128 // heads
+    wide = k_s.shape[1]
+    blocks_w = wide // 128
+
+    def source(shape, axis):
+        place = lax.broadcasted_iota(jnp.int32, shape, axis)
+        block = lax.shift_right_logical(place, 7)
+        spot = place - block * 128
+        head = jnp.zeros(shape, jnp.int32)
+        for number in range(1, heads + 1):
+            head = head + jnp.where(spot >= number * per, 1, 0)
+        dim = block * per + spot - head * per
+        return jnp.where((head < heads) & (dim < DH), head * DH + dim, -1)
+
+    row = lax.broadcasted_iota(jnp.int32, (width, wide), 0)
+    perm[...] = jnp.where(row == source((1, wide), 1), 1.0, 0.0).astype(jnp.bfloat16)
+    col = lax.broadcasted_iota(jnp.int32, (wide, width), 1)
+    unperm[...] = jnp.where(col == source((wide, 1), 0), 1.0, 0.0).astype(jnp.bfloat16)
+
+    def head_of(shape, axis):
+        place = lax.broadcasted_iota(jnp.int32, shape, axis)
+        head = jnp.where(place >= 128, heads + 1, 0)
+        for number in range(1, heads + 1):
+            head = head + jnp.where((place & 127) >= number * per, 1, 0)
+        return jnp.where((place & 127) >= heads * per, -1 - axis, head)
+
+    gather[...] = jnp.where(head_of((256, 1), 0) == head_of((1, 256), 1), 1.0 / DH**0.5, 0.0).astype(
+        jnp.bfloat16
+    )
+    edge = jnp.zeros((pad, wide), jnp.float32)
+    for buffer in (k_s, v_s):
         buffer[0:pad] = edge
         buffer[rows + pad : rows + 2 * pad] = edge
+    for slot, plain, spread in ((8, wq, wqp), (9, wk, wkp), (10, wv, wvp)):
+        stage[slot].wait()
+        spread[...] = jnp.dot(
+            plain[...], perm[...], preferred_element_type=jnp.float32
+        ).astype(jnp.bfloat16)
+    stage[11].wait()
+    wop[...] = jnp.dot(unperm[...], wo[...], preferred_element_type=jnp.float32).astype(
+        jnp.bfloat16
+    )
 
     for slot in (3, 5, 6, 7):
         stage[slot].wait()
@@ -211,8 +255,8 @@
             rate[s * fdev + f] = speed[s : s + 1]
         for slot in range(SPAN):
             offset = slot - BAND
-            valid = ((reach >= -offset) & (spot + offset >= 0) & (spot + offset < frames)).astype(
-                jnp.float32
+            valid = jnp.where(
+                (reach >= -offset) & (spot + offset >= 0) & (spot + offset < frames), 0.0, -1e30
             )
             for s in range(n):
                 mask[slot, s * fdev + f] = valid[s : s + 1]
@@ -227,55 +271,63 @@
         for s in range(n):
             cond[s * fdev + f] = full[s : s + 1]
 
-    for slot in (8, 9, 10, 11):
-        stage[slot].wait()
-
     gain = gain_s[...].reshape(1, 1, width)
-    scale = 1.0 / DH**0.5
-    group = frames // blocks
-    size = group * pos
+    cell = 8
 
     def project(current):
         hin = current + cond[...]
         power = jnp.mean(hin * hin, axis=-1, keepdims=True)
         flat = (hin * lax.rsqrt(power + 1e-06) * gain).reshape(rows, width).astype(jnp.bfloat16)
-        q_s[...] = jnp.dot(flat, wq[...], preferred_element_type=jnp.float32).astype(jnp.bfloat16)
-        fill = jnp.zeros((pos, width), jnp.float32)
-        for weight, even, odd in ((wk, k_even, k_odd), (wv, v_even, v_odd)):
-            made = jnp.dot(flat, weight[...], preferred_element_type=jnp.float32)
-            even[pad : pad + rows] = made.astype(jnp.bfloat16)
-            odd[0 : rows + 2 * pos] = jnp.concatenate([fill, made, fill], axis=0).astype(
-                jnp.bfloat16
+        q_s[...] = jnp.dot(flat, wqp[...], preferred_element_type=jnp.float32)
+        k_s[pad : pad + rows] = jnp.dot(flat, wkp[...], preferred_element_type=jnp.float32)
+        v_s[pad : pad + rows] = jnp.dot(flat, wvp[...], preferred_element_type=jnp.float32)
+
+    def attend(current):
+        size = cell * pos
+        for first in range(0, frames, cell):
+            start = first * pos
+            for slot in range(SPAN):
+                at = start + slot * pos
+                total = None
+                for block in range(blocks_w):
+                    lanes = slice(block * 128, block * 128 + 128)
+                    term = q_s[start : start + size, lanes] * k_s[at : at + size, lanes]
+                    total = term if total is None else total + term
+                part[start : start + size, slot * 128 : slot * 128 + 128] = total.astype(
+                    jnp.bfloat16
+                )
+        raws = []
+        for slot in range(0, SPAN, 2):
+            lanes = min(2, SPAN - slot) * 128
+            made = jnp.dot(
+                part[:, slot * 128 : slot * 128 + lanes],
+                gather[0:lanes, 0:lanes],
+                preferred_element_type=jnp.float32,
             )
-
-    def attend(first, current):
-        at = pl.ds(first, group)
-        start = first * pos
-
-        def shifted(even, odd, slot):
-            source = even if slot % 2 == 0 else odd
-            return source[pl.ds(pl.multiple_of(start + (slot - slot % 2) * pos, 16), size)]
-
-        query = q_s[pl.ds(pl.multiple_of(start, 16), size)]
-        scores = []
-        masks = []
-        for slot in range(SPAN):
-            keys = shifted(k_even, k_odd, slot)
-            raw = jnp.dot(query * keys, fold[...], preferred_element_type=jnp.float32) * scale
-            valid = mask[slot, at]
-            scores.append(jnp.where(valid > 0.0, raw.reshape(group, pos, 128), -1e30))
-            masks.append(valid)
-        top = functools.reduce(jnp.maximum, scores)
-        expo = [jnp.exp(score - top) * valid for score, valid in zip(scores, masks)]
-        inverse = 1.0 / functools.reduce(jnp.add, expo)
-        total = None
-        for slot in range(SPAN):
-            weight = (expo[slot] * inverse).reshape(size, 128).astype(jnp.bfloat16)
-            spread = jnp.dot(weight, unfold[...], preferred_element_type=jnp.float32)
-            term = spread * shifted(v_even, v_odd, slot).astype(jnp.float32)
-            total = term if total is None else total + term
-        noise = jnp.dot(total.astype(jnp.bfloat16), wo[...], preferred_element_type=jnp.float32)
-        return current - rate[at] * noise.reshape(group, pos, width)
+            raws.extend(made[:, at : at + 128] for at in range(0, lanes, 128))
+        for first in range(0, frames, cell):
+            start = first * pos
+            scores = []
+            for slot in range(SPAN):
+                raw = raws[slot][start : start + size].reshape(cell, pos, 128)
+                scores.append(raw + mask[slot, first : first + cell])
+            top = functools.reduce(jnp.maximum, scores)
+            expo = [jnp.exp(score - top) for score in scores]
+            inverse = 1.0 / functools.reduce(jnp.add, expo)
+            weights = [
+                (one * inverse).reshape(size, 128).astype(jnp.bfloat16).astype(jnp.float32)
+                for one in expo
+            ]
+            for block in range(blocks_w):
+                lanes = slice(block * 128, block * 128 + 128)
+                total = None
+                for slot in range(SPAN):
+                    at = start + slot * pos
+                    term = weights[slot] * v_s[at : at + size, lanes]
+                    total = term if total is None else total + term
+                att[start : start + size, lanes] = total.astype(jnp.bfloat16)
+        noise = jnp.dot(att[...], wop[...], preferred_element_type=jnp.float32)
+        return current - rate[...] * noise.reshape(frames, pos, width)
 
     def half(h, carry):
         stage_x = pltpu.make_async_copy(x_hbm.at[:, me, h], recv.at[h, mine], local.at[12 + h])
@@ -298,17 +350,11 @@
 
             project(load(0, frames))
 
-            def body(index, carry, load=load, fresh=fresh, last=last):
-                first = index * group
-                made = attend(first, load(first, group))
-                if last:
-                    xo[h, pl.ds(first, group)] = made.astype(jnp.bfloat16)
-                else:
-                    spot = pl.multiple_of(first * pos + turn, 16)
-                    fresh[pl.ds(spot, size)] = made.reshape(size, width).astype(jnp.bfloat16)
-                return carry
-
-            lax.fori_loop(0, blocks, body, 0)
+            made = attend(load(0, frames))
+            if last:
+                xo[h] = made.astype(jnp.bfloat16)
+            else:
+                fresh[turn : turn + rows] = made.reshape(rows, width).astype(jnp.bfloat16)
             if not last:
                 fresh[0:turn] = fresh[rows : rows + turn]
         for peer in peers:
@@ -340,7 +386,6 @@
 
 
 HALVES = 2
-BLOCKS = 1
 GRANT = 40 << 20
 
 
@@ -370,10 +415,11 @@
     dma = pltpu.SemaphoreType.DMA
     block = pltpu.VMEM((HALVES, frames, pos, width), bf16)
     rolled = pltpu.VMEM((rows + fdev * pos, width), bf16)
-    padded = pltpu.VMEM((rows + 2 * BAND * pos, width), bf16)
+    wide = -(-DH // (128 // (width // DH))) * 128
+    padded = pltpu.VMEM((rows + 2 * BAND * pos, wide), f32)
     square = pltpu.VMEM((width, width), bf16)
     out = pl.pallas_call(
-        functools.partial(queue_kernel, n, BLOCKS),
+        functools.partial(queue_kernel, n),
         out_shape=jax.ShapeDtypeStruct((fdev, n, HALVES, pos, width), bf16),
         in_specs=[stored] * 13,
         out_specs=anywhere,
@@ -382,11 +428,11 @@
             rolled,
             rolled,
             block,
-            pltpu.VMEM((rows, width), bf16),
+            pltpu.VMEM((rows, wide), f32),
             padded,
             padded,
-            padded,
-            padded,
+            pltpu.VMEM((rows, SPAN * 128), bf16),
+            pltpu.VMEM((rows, wide), bf16),
             pltpu.VMEM(text_table.shape, bf16),
             pltpu.VMEM(text_proj.shape, bf16),
             pltpu.VMEM(level_embed.shape, f32),
@@ -395,6 +441,10 @@
             square,
             square,
             square,
+            pltpu.VMEM((width, wide), bf16),
+            pltpu.VMEM((width, wide), bf16),
+            pltpu.VMEM((width, wide), bf16),
+            pltpu.VMEM((wide, width), bf16),
             pltpu.SMEM(levels.shape, i32),
             pltpu.SMEM(back_reach.shape, i32),
             pltpu.SMEM(text_ids.shape, i32),
@@ -404,8 +454,9 @@
             pltpu.VMEM((frames, 1, width), f32),
             pltpu.VMEM((frames, 1, width), f32),
             pltpu.VMEM((SPAN, frames, 1, 128), f32),
-            pltpu.VMEM((width, 128), bf16),
-            pltpu.VMEM((128, width), bf16),
+            pltpu.VMEM((width, wide), bf16),
+            pltpu.VMEM((wide, width), bf16),
+            pltpu.VMEM((256, 256), bf16),
             dma((HALVES, n)),
             dma((HALVES, n)),
             dma((n,)),
@@ -518,7 +569,8 @@
 def per_device(latents, *rest):
     n = lax.axis_size("level")
     tokens = latents.shape[1]
-    if tokens % (8 * HALVES * n) == 0 and latents.shape[0] % 2 == 0:
+    fits = tokens % (8 * HALVES * n) == 0 and latents.shape[0] * n % 8 == 0
+    if fits and n & (n - 1) == 0:
         return fused(latents, *rest)
     return general(latents, *rest)
 

time: 44.4 us -> 44.3 us (level)
  no operation moved by 1% of the time
where the time goes in v1:
time: 44.3 us; the launch traced here: 44.2 us
  Pallas kernels  43.3 us (98%)
  local copies, waits for them, and re-layouts  0.84 us (2%)
    pallas_call x1, Pallas kernels, fused(): pl.pallas_call(functools.partial(queue_kernel, n), out_shape=jax.ShapeDty...  43.3 us

profile of v1, /device:TPU:0, one launch (start us, length us, event | category | flops | bytes accessed | tf_op | source)
XLA Modules:
  0.0 44.2 jit_solution(720168297736784272)
XLA Ops:
  0.0 43.3 %queue.1 = bf16[2,16,2,8,640]{4,3,2,1,0:T(8,128)(2,1)S(1)} custom-call(bf16[2,16,2,8,640]{4,3,2,1,0:T(8,128)(2,1)} %bitcast.3, s32[2]{0:T(128)} %level_hbm.1, s32[2]{0:T(128)} %reach_hbm.1, s32[77]{0:T(128)} %ids_hbm.1, bf16[3088,1024]{1,0:T(8,128)(2,1)} %table_hbm.1, bf16[1024,640]{1,0:T(8,128)(2,1)} %proj_hbm.1, f32[16,640]{1,0:T(8,128)} %embed_hbm.1, ...), custom_call_target="tpu_custom_call" | custom-call | tf_op jit(solution)/shard_map/queue/pallas_call | solution.py:421
  43.3 0.8 %copy.15 = bf16[2,256,640]{2,1,0:T(8,128)(2,1)} copy(bf16[2,256,640]{2,1,0:T(8,128)(2,1)S(1)} %bitcast.2) | data formatting | bytes 1310720

commit v2 on v1

--- a/solution.py
+++ b/solution.py
@@ -43,13 +43,9 @@
     proj,
     embed,
     gain_s,
-    wq,
-    wk,
-    wv,
+    plain,
     wo,
-    wqp,
-    wkp,
-    wvp,
+    spread,
     wop,
     level_s,
     reach_s,
@@ -57,6 +53,7 @@
     srate_s,
     pool,
     metas,
+    metas_s,
     cond,
     rate,
     mask,
@@ -93,9 +90,9 @@
         (embed_hbm, embed),
         (gain_hbm, gain_s),
         (proj_hbm, proj),
-        (wq_hbm, wq),
-        (wk_hbm, wk),
-        (wv_hbm, wv),
+        (wq_hbm, plain.at[0]),
+        (wk_hbm, plain.at[1]),
+        (wv_hbm, plain.at[2]),
         (wo_hbm, wo),
     ] + [(x_hbm.at[:, me, h], recv.at[h, mine]) for h in range(halves)]
     stage = [
@@ -152,9 +149,11 @@
                 other = other + (1 - 2 * bit) * (1 << place)
         return other
 
-    peers = [flip(bits) for bits in range(1, n)]
+    first = [bits for bits in (8, 12, 9, 4, 1, 2, 5, 3) if bits < n]
+    order = first + [bits for bits in range(n - 1, 0, -1) if bits not in first]
+    peers = [flip(bits) for bits in order]
     pl.semaphore_wait(barrier, n - 1)
-    early = n // 2
+    early = len(first)
     for peer in peers[:early]:
         x_copy(0, peer, me).start()
 
@@ -172,15 +171,21 @@
     vocab = table.shape[0]
     stage[2].wait()
     first_id = me * vocab
-    spots = lax.broadcasted_iota(jnp.int32, (1, vocab), 1) + first_id
-    counts = jnp.zeros((1, vocab), jnp.float32)
     text_tokens = ids_s.shape[0]
-    for token in range(text_tokens):
-        counts = counts + jnp.where(spots == ids_s[token], 1.0, 0.0)
-    counts = jnp.broadcast_to(counts, (16, vocab)).astype(jnp.bfloat16)
+    sublane = lax.broadcasted_iota(jnp.int32, (8, 1), 0)
+    spots = lax.broadcasted_iota(jnp.int32, (8, vocab), 1)
+    counts = jnp.zeros((8, vocab), jnp.float32)
+    for first_token in range(0, text_tokens, 8):
+        wanted = jnp.full((8, 1), -1, jnp.int32)
+        for token in range(first_token, min(first_token + 8, text_tokens)):
+            wanted = jnp.where(sublane == token - first_token, ids_s[token] - first_id, wanted)
+        counts = counts + jnp.where(spots == wanted, 1.0, 0.0)
+    counts = jnp.concatenate([counts, jnp.zeros((8, vocab), jnp.float32)], axis=0).astype(
+        jnp.bfloat16
+    )
     stage[4].wait()
     partial = jnp.dot(counts, table[...], preferred_element_type=jnp.float32)
-    pool[me] = partial[0:1]
+    pool[me] = jnp.sum(partial[0:8], axis=0, keepdims=True)
     for peer in peers:
         p_copy(peer, me).start()
     for peer in peers[early:]:
@@ -194,20 +199,33 @@
     wide = k_s.shape[1]
     blocks_w = wide // 128
 
-    def source(shape, axis):
-        place = lax.broadcasted_iota(jnp.int32, shape, axis)
+    def source(place):
         block = lax.shift_right_logical(place, 7)
         spot = place - block * 128
-        head = jnp.zeros(shape, jnp.int32)
+        head = jnp.zeros(place.shape, jnp.int32)
         for number in range(1, heads + 1):
             head = head + jnp.where(spot >= number * per, 1, 0)
         dim = block * per + spot - head * per
         return jnp.where((head < heads) & (dim < DH), head * DH + dim, -1)
 
-    row = lax.broadcasted_iota(jnp.int32, (width, wide), 0)
-    perm[...] = jnp.where(row == source((1, wide), 1), 1.0, 0.0).astype(jnp.bfloat16)
-    col = lax.broadcasted_iota(jnp.int32, (wide, width), 1)
-    unperm[...] = jnp.where(col == source((wide, 1), 0), 1.0, 0.0).astype(jnp.bfloat16)
+    strip = 64
+
+    def build_perm(index, carry):
+        at = pl.multiple_of(index * strip, strip)
+        row = lax.broadcasted_iota(jnp.int32, (strip, wide), 0) + at
+        here = row == source(lax.broadcasted_iota(jnp.int32, (1, wide), 1))
+        perm[pl.ds(at, strip)] = jnp.where(here, 1.0, 0.0).astype(jnp.bfloat16)
+        return carry
+
+    def build_unperm(index, carry):
+        at = pl.multiple_of(index * strip, strip)
+        col = lax.broadcasted_iota(jnp.int32, (strip, width), 1)
+        here = col == source(lax.broadcasted_iota(jnp.int32, (strip, 1), 0) + at)
+        unperm[pl.ds(at, strip)] = jnp.where(here, 1.0, 0.0).astype(jnp.bfloat16)
+        return carry
+
+    lax.fori_loop(0, width // strip, build_perm, 0)
+    lax.fori_loop(0, wide // strip, build_unperm, 0)
 
     def head_of(shape, axis):
         place = lax.broadcasted_iota(jnp.int32, shape, axis)
@@ -223,53 +241,48 @@
     for buffer in (k_s, v_s):
         buffer[0:pad] = edge
         buffer[rows + pad : rows + 2 * pad] = edge
-    for slot, plain, spread in ((8, wq, wqp), (9, wk, wkp), (10, wv, wvp)):
+    for peer in peers:
+        m_copy(peer, peer).wait_recv()
+    told = pltpu.make_async_copy(metas, metas_s, local.at[12 + 2 * halves])
+    told.start()
+    for slot in (8, 9, 10, 11):
         stage[slot].wait()
-        spread[...] = jnp.dot(
-            plain[...], perm[...], preferred_element_type=jnp.float32
+
+    def respread(index, carry):
+        spread[index] = jnp.dot(
+            plain[index], perm[...], preferred_element_type=jnp.float32
         ).astype(jnp.bfloat16)
-    stage[11].wait()
+        return carry
+
+    lax.fori_loop(0, 3, respread, 0)
     wop[...] = jnp.dot(unperm[...], wo[...], preferred_element_type=jnp.float32).astype(
         jnp.bfloat16
     )
 
     for slot in (3, 5, 6, 7):
         stage[slot].wait()
-    for peer in peers:
-        m_copy(peer, peer).wait_recv()
-    facts = metas[...].reshape(n, 128)
-    slot_index = lax.broadcasted_iota(jnp.int32, (n, 128), 0)
-    bases = []
-    for f in range(fdev):
-        level = facts[:, f : f + 1]
-        base = jnp.zeros((n, width), jnp.float32)
-        speed = jnp.zeros((n, width), jnp.float32)
-        for number in range(embed.shape[0]):
-            chosen = level == number
-            base = base + jnp.where(chosen, embed[number : number + 1, :], 0.0)
-            speed = speed + jnp.where(chosen, srate_s[number], 0.0)
-        bases.append(base)
-        reach = jnp.broadcast_to(facts[:, fdev + f : fdev + f + 1], (n, 128))
-        spot = slot_index * fdev + f
-        for s in range(n):
-            rate[s * fdev + f] = speed[s : s + 1]
+    told.wait()
+    for frame in range(frames):
+        s, f = divmod(frame, fdev)
+        level = metas_s[s, 0, f]
+        reach = metas_s[s, 0, fdev + f]
+        rate[frame] = jnp.full((1, width), srate_s[level], jnp.float32)
+        cond[frame] = embed[pl.ds(level, 1), :]
         for slot in range(SPAN):
             offset = slot - BAND
-            valid = jnp.where(
-                (reach >= -offset) & (spot + offset >= 0) & (spot + offset < frames), 0.0, -1e30
-            )
-            for s in range(n):
-                mask[slot, s * fdev + f] = valid[s : s + 1]
+            inside = 0 <= frame + offset < frames
+            if offset < 0 and inside:
+                value = jnp.where(reach >= -offset, 0.0, -1e30)
+            else:
+                value = 0.0 if inside else -1e30
+            mask[slot, frame] = jnp.full((1, 128), value, jnp.float32)
 
     for peer in peers:
         p_copy(peer, peer).wait_recv()
     pooled = jnp.sum(pool[...], axis=0) / float(text_tokens)
     pooled = jnp.broadcast_to(pooled, (16, pooled.shape[1])).astype(jnp.bfloat16)
     text = jnp.dot(pooled, proj[...], preferred_element_type=jnp.float32)[0:1]
-    for f in range(fdev):
-        full = bases[f] + text
-        for s in range(n):
-            cond[s * fdev + f] = full[s : s + 1]
+    cond[...] = cond[...] + text.reshape(1, 1, width)
 
     gain = gain_s[...].reshape(1, 1, width)
     cell = 8
@@ -278,9 +291,9 @@
         hin = current + cond[...]
         power = jnp.mean(hin * hin, axis=-1, keepdims=True)
         flat = (hin * lax.rsqrt(power + 1e-06) * gain).reshape(rows, width).astype(jnp.bfloat16)
-        q_s[...] = jnp.dot(flat, wqp[...], preferred_element_type=jnp.float32)
-        k_s[pad : pad + rows] = jnp.dot(flat, wkp[...], preferred_element_type=jnp.float32)
-        v_s[pad : pad + rows] = jnp.dot(flat, wvp[...], preferred_element_type=jnp.float32)
+        q_s[...] = jnp.dot(flat, spread[0], preferred_element_type=jnp.float32)
+        k_s[pad : pad + rows] = jnp.dot(flat, spread[1], preferred_element_type=jnp.float32)
+        v_s[pad : pad + rows] = jnp.dot(flat, spread[2], preferred_element_type=jnp.float32)
 
     def attend(current):
         size = cell * pos
@@ -437,13 +450,9 @@
             pltpu.VMEM(text_proj.shape, bf16),
             pltpu.VMEM(level_embed.shape, f32),
             pltpu.VMEM(norm_gain.shape, f32),
+            pltpu.VMEM((3, width, width), bf16),
             square,
-            square,
-            square,
-            square,
-            pltpu.VMEM((width, wide), bf16),
-            pltpu.VMEM((width, wide), bf16),
-            pltpu.VMEM((width, wide), bf16),
+            pltpu.VMEM((3, width, wide), bf16),
             pltpu.VMEM((wide, width), bf16),
             pltpu.SMEM(levels.shape, i32),
             pltpu.SMEM(back_reach.shape, i32),
@@ -451,6 +460,7 @@
             pltpu.SMEM(step_rate.shape, f32),
             pltpu.VMEM((n, 1, text_table.shape[1]), f32),
             pltpu.VMEM((n, 1, 128), i32),
+            pltpu.SMEM((n, 1, 128), i32),
             pltpu.VMEM((frames, 1, width), f32),
             pltpu.VMEM((frames, 1, width), f32),
             pltpu.VMEM((SPAN, frames, 1, 128), f32),
@@ -465,7 +475,7 @@
             dma((n,)),
             dma((HALVES, n)),
             dma((HALVES, n)),
-            dma((12 + 2 * HALVES,)),
+            dma((13 + 2 * HALVES,)),
         ],
         compiler_params=pltpu.CompilerParams(
             collective_id=0, has_side_effects=True, vmem_limit_bytes=GRANT

time: 44.3 us -> 43.4 us (0.980)
  Pallas kernels: 43.3 us -> 42.4 us
    pallas_call x1, Pallas kernels: 43.3 us -> 42.4 us  [fused(): pl.pallas_call(functools.partial(queue_kernel, n), out_shape=jax.ShapeDty...]
where the time goes in v2:
time: 43.4 us; the launch traced here: 43.3 us
  Pallas kernels  42.4 us (98%)
  local copies, waits for them, and re-layouts  0.84 us (2%)
    pallas_call x1, Pallas kernels, fused(): pl.pallas_call(functools.partial(queue_kernel, n), out_shape=jax.ShapeDty...  42.4 us

profile of v2, /device:TPU:0, one launch (start us, length us, event | category | flops | bytes accessed | tf_op | source)
XLA Modules:
  0.0 43.3 jit_solution(14715851873035698451)
XLA Ops:
  0.0 42.4 %queue.1 = bf16[2,16,2,8,640]{4,3,2,1,0:T(8,128)(2,1)S(1)} custom-call(bf16[2,16,2,8,640]{4,3,2,1,0:T(8,128)(2,1)} %bitcast.3, s32[2]{0:T(128)} %level_hbm.1, s32[2]{0:T(128)} %reach_hbm.1, s32[77]{0:T(128)} %ids_hbm.1, bf16[3088,1024]{1,0:T(8,128)(2,1)} %table_hbm.1, bf16[1024,640]{1,0:T(8,128)(2,1)} %proj_hbm.1, f32[16,640]{1,0:T(8,128)} %embed_hbm.1, ...), custom_call_target="tpu_custom_call" | custom-call | tf_op jit(solution)/shard_map/queue/pallas_call | solution.py:434
  42.4 0.8 %copy.15 = bf16[2,256,640]{2,1,0:T(8,128)(2,1)} copy(bf16[2,256,640]{2,1,0:T(8,128)(2,1)S(1)} %bitcast.2) | data formatting | bytes 1310720

commit v3 on v2

--- a/solution.py
+++ b/solution.py
@@ -149,11 +149,10 @@
                 other = other + (1 - 2 * bit) * (1 << place)
         return other
 
-    first = [bits for bits in (8, 12, 9, 4, 1, 2, 5, 3) if bits < n]
-    order = first + [bits for bits in range(n - 1, 0, -1) if bits not in first]
+    order = sorted(range(1, n), key=lambda bits: (bits < 4, not bits & 2, bits))
     peers = [flip(bits) for bits in order]
     pl.semaphore_wait(barrier, n - 1)
-    early = len(first)
+    early = 4
     for peer in peers[:early]:
         x_copy(0, peer, me).start()
 
@@ -241,10 +240,6 @@
     for buffer in (k_s, v_s):
         buffer[0:pad] = edge
         buffer[rows + pad : rows + 2 * pad] = edge
-    for peer in peers:
-        m_copy(peer, peer).wait_recv()
-    told = pltpu.make_async_copy(metas, metas_s, local.at[12 + 2 * halves])
-    told.start()
     for slot in (8, 9, 10, 11):
         stage[slot].wait()
 
@@ -259,6 +254,10 @@
         jnp.bfloat16
     )
 
+    for peer in peers:
+        m_copy(peer, peer).wait_recv()
+    told = pltpu.make_async_copy(metas, metas_s, local.at[12 + 2 * halves])
+    told.start()
     for slot in (3, 5, 6, 7):
         stage[slot].wait()
     told.wait()

time: 43.4 us -> 42.6 us (0.982)
  Pallas kernels: 42.4 us -> 41.6 us
    pallas_call x1, Pallas kernels: 42.4 us -> 41.6 us  [fused(): pl.pallas_call(functools.partial(queue_kernel, n), out_shape=jax.ShapeDty...]
where the time goes in v3:
time: 42.6 us; the launch traced here: 42.5 us
  Pallas kernels  41.6 us (98%)
  local copies, waits for them, and re-layouts  0.84 us (2%)
    pallas_call x1, Pallas kernels, fused(): pl.pallas_call(functools.partial(queue_kernel, n), out_shape=jax.ShapeDty...  41.6 us

profile of v3, /device:TPU:0, one launch (start us, length us, event | category | flops | bytes accessed | tf_op | source)
XLA Modules:
  0.0 42.5 jit_solution(8389192291780786937)
XLA Ops:
  0.0 41.6 %queue.1 = bf16[2,16,2,8,640]{4,3,2,1,0:T(8,128)(2,1)S(1)} custom-call(bf16[2,16,2,8,640]{4,3,2,1,0:T(8,128)(2,1)} %bitcast.3, s32[2]{0:T(128)} %level_hbm.1, s32[2]{0:T(128)} %reach_hbm.1, s32[77]{0:T(128)} %ids_hbm.1, bf16[3088,1024]{1,0:T(8,128)(2,1)} %table_hbm.1, bf16[1024,640]{1,0:T(8,128)(2,1)} %proj_hbm.1, f32[16,640]{1,0:T(8,128)} %embed_hbm.1, ...), custom_call_target="tpu_custom_call" | custom-call | tf_op jit(solution)/shard_map/queue/pallas_call | solution.py:433
  41.6 0.8 %copy.15 = bf16[2,256,640]{2,1,0:T(8,128)(2,1)} copy(bf16[2,256,640]{2,1,0:T(8,128)(2,1)S(1)} %bitcast.2) | data formatting | bytes 1310720

commit v4 on v3

--- a/solution.py
+++ b/solution.py
@@ -189,9 +189,6 @@
         p_copy(peer, me).start()
     for peer in peers[early:]:
         x_copy(0, peer, me).start()
-    for h in range(1, halves):
-        for peer in peers:
-            x_copy(h, peer, me).start()
 
     heads = width // DH
     per = 128 // heads
@@ -250,6 +247,9 @@
         return carry
 
     lax.fori_loop(0, 3, respread, 0)
+    for h in range(1, halves):
+        for peer in peers:
+            x_copy(h, peer, me).start()
     wop[...] = jnp.dot(unperm[...], wo[...], preferred_element_type=jnp.float32).astype(
         jnp.bfloat16
     )

time: 42.6 us -> 42.6 us (level)
  no operation moved by 1% of the time
where the time goes in v4:
time: 42.6 us; the launch traced here: 42.5 us
  Pallas kernels  41.6 us (98%)
  local copies, waits for them, and re-layouts  0.84 us (2%)
    pallas_call x1, Pallas kernels, fused(): pl.pallas_call(functools.partial(queue_kernel, n), out_shape=jax.ShapeDty...  41.6 us

profile of v4, /device:TPU:0, one launch (start us, length us, event | category | flops | bytes accessed | tf_op | source)
XLA Modules:
  0.0 42.5 jit_solution(12916979172820199561)
XLA Ops:
  0.0 41.6 %queue.1 = bf16[2,16,2,8,640]{4,3,2,1,0:T(8,128)(2,1)S(1)} custom-call(bf16[2,16,2,8,640]{4,3,2,1,0:T(8,128)(2,1)} %bitcast.3, s32[2]{0:T(128)} %level_hbm.1, s32[2]{0:T(128)} %reach_hbm.1, s32[77]{0:T(128)} %ids_hbm.1, bf16[3088,1024]{1,0:T(8,128)(2,1)} %table_hbm.1, bf16[1024,640]{1,0:T(8,128)(2,1)} %proj_hbm.1, f32[16,640]{1,0:T(8,128)} %embed_hbm.1, ...), custom_call_target="tpu_custom_call" | custom-call | tf_op jit(solution)/shard_map/queue/pallas_call | solution.py:433
  41.6 0.8 %copy.15 = bf16[2,256,640]{2,1,0:T(8,128)(2,1)} copy(bf16[2,256,640]{2,1,0:T(8,128)(2,1)S(1)} %bitcast.2) | data formatting | bytes 1310720
